TPU v7x, 32 devices: a whole 2x2x4 slice. The times are simulated.
32 devices in a mesh: seq: 16 (over z, y, core), mp: 2 (over x).
Axes of the slice: x: 2, y: 2, z: 4, core: 2. Of those that a mesh axis runs over, the one named last changes fastest.
Arguments:
- tokens: float32 [8192, 1024], P('seq'), may hold values from -6 to 6
- window_state: float32 [2, 1024, 16], P(None, ('seq', 'mp')), may hold values from -6 to 6
- norm1_gain: float32 [1024], replicated, may hold values from 0.5 to 1.5
- norm1_bias: float32 [1024], replicated, may hold values from -3 to 3
- in_coef: float32 [1024, 16], P(('seq', 'mp')), may hold values from -0.375 to 0.375
- out_coef: float32 [1024, 16], P(('seq', 'mp')), may hold values from -4 to 4
- decay_rate: float32 [1024, 16], P(('seq', 'mp')), may hold values from 6.1035156e-05 to 0.04
- skip_gain: float32 [1024], P(('seq', 'mp')), may hold values from 0.5 to 1.5
- qkv_weight: bfloat16 [3, 1024, 1024], P(None, None, 'mp'), may hold values from -0.1875 to 0.1875
- out_weight: bfloat16 [1024, 1024], P('mp'), may hold values from -0.75 to 0.75
- norm2_gain: float32 [1024], replicated, may hold values from 0.5 to 1.5
- norm2_bias: float32 [1024], replicated, may hold values from -3 to 3
- up_weight: bfloat16 [1024, 4096], P(None, 'mp'), may hold values from -0.1875 to 0.1875
- up_bias: float32 [4096], P('mp'), may hold values from -3 to 3
- down_weight: bfloat16 [4096, 1024], P('mp'), may hold values from -0.1875 to 0.1875
- down_bias: float32 [1024], replicated, may hold values from -3 to 3
- cotangent: float32 [8192, 1024], P('seq'), may hold values from -6 to 6
Outputs:
- result: float32 [8192, 1024], P('seq')
- grad_tokens: float32 [8192, 1024], P('seq')
- grad_norm1_gain: float32 [1024], replicated
- grad_norm1_bias: float32 [1024], replicated
- grad_in_coef: float32 [1024, 16], P(('seq', 'mp'))
- grad_out_coef: float32 [1024, 16], P(('seq', 'mp'))
- grad_decay_rate: float32 [1024, 16], P(('seq', 'mp'))
- grad_skip_gain: float32 [1024], P(('seq', 'mp'))
- grad_qkv_weight: float32 [3, 1024, 1024], P(None, None, 'mp')
- grad_out_weight: float32 [1024, 1024], P('mp')
- grad_norm2_gain: float32 [1024], replicated
- grad_norm2_bias: float32 [1024], replicated
- grad_up_weight: float32 [1024, 4096], P(None, 'mp')
- grad_up_bias: float32 [4096], P('mp')
- grad_down_weight: float32 [4096, 1024], P('mp')
- grad_down_bias: float32 [1024], replicated
All inputs are finite; a program needn't handle non-finite values.
Results may differ from a plain program's by a relative error of at most 0.002.
Values sent between devices are 32-bit elements; how exact they have to be, the bound alone decides.
No kernel may reach another device: no remote copies, remote signals or barrier semaphores. Data moves between devices by JAX's collectives and lax.ppermute only.
A program may use at most 192 MiB of HBM per device.

v0:
```python
import math
import jax
import jax.numpy as jnp
from jax import lax
from jax.sharding import PartitionSpec as P

HDIM = 128
BLOCK = 512
CTX = 128
LEN = 4096
epsilon = 1e-05


def from_behind(block, axis, distance):
    devices = range(lax.axis_size(axis))
    route = [(i - distance, i) for i in devices if i - distance in devices]
    return lax.ppermute(block, axis, route)


def product(form, left, right):
    return jnp.einsum(form, left, right, precision=lax.Precision.HIGHEST)


def layer_norm(value, gain, bias):
    center = value - jnp.mean(value, axis=-1, keepdims=True)
    spread = jnp.mean(center * center, axis=-1, keepdims=True)
    return center * lax.rsqrt(spread + epsilon) * gain + bias


def angle_table(count_rows, count_cols, modulus):
    left = jnp.arange(count_rows, dtype=jnp.int32)[:, None]
    right = jnp.arange(count_cols, dtype=jnp.int32)[None, :]
    phase = left * right % modulus
    angle = phase.astype(jnp.float32) * (2.0 * math.pi / modulus)
    return (jnp.cos(angle), jnp.sin(angle))


def forward_dft(signal, tables):
    cos_one, sin_one, cos_twid, sin_twid, cos_two, sin_two = tables
    first_re = product("...ab,ak->...kb", signal, cos_one)
    first_im = -product("...ab,ak->...kb", signal, sin_one)
    twid_re = first_re * cos_twid + first_im * sin_twid
    twid_im = first_im * cos_twid - first_re * sin_twid
    spec_re = product("...kb,bm->...km", twid_re, cos_two) + product(
        "...kb,bm->...km", twid_im, sin_two
    )
    spec_im = product("...kb,bm->...km", twid_im, cos_two) - product(
        "...kb,bm->...km", twid_re, sin_two
    )
    return (spec_re, spec_im)


def inverse_dft(spec_re, spec_im, tables, total):
    cos_one, sin_one, cos_twid, sin_twid, cos_two, sin_two = tables
    back_re = product("...km,mb->...kb", spec_re, cos_two) - product(
        "...km,mb->...kb", spec_im, sin_two
    )
    back_im = product("...km,mb->...kb", spec_re, sin_two) + product(
        "...km,mb->...kb", spec_im, cos_two
    )
    turn_re = back_re * cos_twid - back_im * sin_twid
    turn_im = back_re * sin_twid + back_im * cos_twid
    real_part = product("...kb,ka->...ab", turn_re, cos_one) - product(
        "...kb,ka->...ab", turn_im, sin_one
    )
    return real_part / total


def causal_conv(signal, kernel):
    channels, windows, length = signal.shape
    total = 2 * length
    bits = total.bit_length() - 1
    cols_count = 1 << bits - bits // 2
    rows_count = total // cols_count
    cos_one, sin_one = angle_table(rows_count, rows_count, rows_count)
    cos_twid, sin_twid = angle_table(rows_count, cols_count, total)
    cos_two, sin_two = angle_table(cols_count, cols_count, cols_count)
    tables = (cos_one, sin_one, cos_twid, sin_twid, cos_two, sin_two)
    padded = jnp.concatenate([signal, jnp.zeros_like(signal)], -1).reshape(
        channels, windows, rows_count, cols_count
    )
    kern_pad = jnp.concatenate([kernel, jnp.zeros_like(kernel)], -1).reshape(
        channels, 1, rows_count, cols_count
    )
    sig_re, sig_im = forward_dft(padded, tables)
    ker_re, ker_im = forward_dft(kern_pad, tables)
    prod_re = sig_re * ker_re - sig_im * ker_im
    prod_im = sig_re * ker_im + sig_im * ker_re
    whole = inverse_dft(prod_re, prod_im, tables, total).reshape(channels, windows, total)
    return whole[:, :, :length]


def ssm_local(time_rows, in_coef, out_coef, decay_rate, skip_gain, window_state):
    channels = time_rows.shape[0]
    windows = time_rows.shape[1] // LEN
    signal = time_rows.reshape(channels, windows, LEN)
    steps_t = jnp.arange(LEN).astype(jnp.float32)
    fading = jnp.exp(-decay_rate[:, :, None] * steps_t)
    kernel = product("cn,cnt->ct", in_coef * out_coef, fading)
    shifted = fading * jnp.exp(-decay_rate)[:, :, None]
    start = jnp.einsum(
        "cn,scn,cnt->cst", out_coef, window_state, shifted, precision=lax.Precision.HIGHEST
    )
    conv = causal_conv(signal, kernel)
    return (conv + skip_gain[:, None, None] * signal + start).reshape(channels, windows * LEN)


def attend_local(normed, context, qkv, out_w, ctx_ok):
    rows_here, model_width = normed.shape
    inner = qkv.shape[2]
    blocks = rows_here // BLOCK
    heads_here = inner // HDIM
    highest = lax.Precision.HIGHEST
    query = jnp.dot(normed, qkv[0], precision=highest).reshape(blocks, BLOCK, heads_here, HDIM)
    key_self = jnp.dot(normed, qkv[1], precision=highest).reshape(blocks, BLOCK, heads_here, HDIM)
    value_self = jnp.dot(normed, qkv[2], precision=highest).reshape(blocks, BLOCK, heads_here, HDIM)
    key_ctx = product("dbc,de->bce", context, qkv[1]).reshape(blocks, CTX, heads_here, HDIM)
    value_ctx = product("dbc,de->bce", context, qkv[2]).reshape(blocks, CTX, heads_here, HDIM)
    keys = jnp.concatenate([key_ctx, key_self], 1)
    values = jnp.concatenate([value_ctx, value_self], 1)
    scores = product("bqhe,bkhe->bhqk", query, keys) * HDIM ** (-0.5)
    rows_q = jnp.arange(BLOCK)[:, None]
    cols_k = jnp.arange(CTX + BLOCK)[None, :]
    allowed = jnp.where(
        cols_k < CTX, ctx_ok[:, None, None, None], (cols_k - CTX <= rows_q)[None, None]
    )
    scores = jnp.where(allowed, scores, -1e30)
    probs = jax.nn.softmax(scores, axis=-1)
    heads = product("bhqk,bkhe->bqhe", probs, values).reshape(rows_here, inner)
    return jnp.dot(heads, out_w, precision=highest)


def feed_local(normed2, up_w, up_b, down_w):
    highest = lax.Precision.HIGHEST
    hidden = jax.nn.gelu(jnp.dot(normed2, up_w, precision=highest) + up_b, approximate=False)
    return jnp.dot(hidden, down_w, precision=highest)


def sum_feed_grads(grad_up, grad_up_bias, grad_down, grad_down_bias):
    return lax.psum((grad_up, grad_up_bias, grad_down, grad_down_bias), "seq")


def per_device(
    tokens,
    window_state,
    norm1_gain,
    norm1_bias,
    in_coef,
    out_coef,
    decay_rate,
    skip_gain,
    qkv_weight,
    out_weight,
    norm2_gain,
    norm2_bias,
    up_weight,
    up_bias,
    down_weight,
    down_bias,
    cotangent,
):
    count_seq = lax.axis_size("seq")
    count_mp = lax.axis_size("mp")
    place_seq = lax.axis_index("seq")
    place_mp = lax.axis_index("mp")
    rows_here, model_width = tokens.shape
    blocks_here = rows_here // BLOCK
    channels = in_coef.shape[0]
    qkv_full = qkv_weight.astype(jnp.float32)
    out_full = out_weight.astype(jnp.float32)
    up_full = up_weight.astype(jnp.float32)
    down_full = down_weight.astype(jnp.float32)
    normed, norm1_pull = jax.vjp(layer_norm, tokens, norm1_gain, norm1_bias)
    grouped = normed.reshape(rows_here, count_seq, count_mp, channels)
    own_half = lax.dynamic_index_in_dim(grouped, place_mp, axis=2, keepdims=False)
    outgoing = jnp.transpose(own_half, (1, 2, 0)).reshape(count_seq * channels, rows_here)
    time_in = lax.all_to_all(outgoing, "seq", split_axis=0, concat_axis=1, tiled=True)

    def ssm_piece(time_rows, coef_in, coef_out, rates, skips):
        return ssm_local(time_rows, coef_in, coef_out, rates, skips, window_state)

    time_out, ssm_pull = jax.vjp(ssm_piece, time_in, in_coef, out_coef, decay_rate, skip_gain)
    returned = lax.all_to_all(time_out, "seq", split_axis=1, concat_axis=0, tiled=True)
    width_back = returned.shape[1]
    halves = lax.all_gather(
        returned.reshape(count_seq, 1, channels, width_back), "mp", axis=1, tiled=True
    )
    joined = halves.reshape(model_width, width_back)
    tail = from_behind(joined[:, rows_here - CTX :], "seq", 1)
    extended = jnp.concatenate([tail, joined], 1)
    context = extended[:, :rows_here].reshape(model_width, blocks_here, BLOCK)[:, :, :CTX]
    block_start = (place_seq * rows_here + jnp.arange(blocks_here) * BLOCK) % LEN
    ctx_ok = block_start > 0

    def attend_piece(normed_in, context_in, qkv_in, out_in):
        return attend_local(normed_in, context_in, qkv_in, out_in, ctx_ok)

    attn_part = attend_piece(normed, context, qkv_full, out_full)
    mixed = tokens + lax.psum(attn_part, "mp")
    normed2, norm2_pull = jax.vjp(layer_norm, mixed, norm2_gain, norm2_bias)
    feed_part = feed_local(normed2, up_full, up_bias, down_full)
    result = mixed + lax.psum(feed_part, "mp") + down_bias
    grad_down_bias = jnp.sum(cotangent, axis=0)
    unused_feed, feed_pull = jax.vjp(feed_local, normed2, up_full, up_bias, down_full)
    grad_normed2_part, grad_up, grad_up_bias, grad_down = feed_pull(cotangent)
    grad_normed2 = lax.psum(grad_normed2_part, "mp")
    grad_mixed_norm, grad_gain2, grad_bias2 = norm2_pull(grad_normed2)
    grad_mixed = cotangent + grad_mixed_norm
    unused_attn, attend_pull = jax.vjp(attend_piece, normed, context, qkv_full, out_full)
    grad_normed_part, grad_context, grad_qkv, grad_out = attend_pull(grad_mixed)
    spread_rows = jnp.pad(grad_context, ((0, 0), (0, 0), (0, BLOCK - CTX))).reshape(
        model_width, rows_here
    )
    grad_extended = jnp.concatenate([spread_rows, jnp.zeros((model_width, CTX), jnp.float32)], 1)
    grad_tail = from_behind(grad_extended[:, :CTX], "seq", -1)
    grad_joined = grad_extended[:, CTX:] + jnp.pad(grad_tail, ((0, 0), (rows_here - CTX, 0)))
    width_grad = grad_joined.shape[1]
    grad_half = lax.psum_scatter(
        grad_joined.reshape(count_seq, count_mp, channels, width_grad),
        "mp",
        scatter_dimension=1,
        tiled=True,
    )
    grad_time = lax.all_to_all(
        grad_half.reshape(count_seq * channels, width_grad),
        "seq",
        split_axis=0,
        concat_axis=1,
        tiled=True,
    )
    grad_time_in, grad_in_coef, grad_out_coef, grad_decay, grad_skip = ssm_pull(grad_time)
    grad_back = lax.all_to_all(grad_time_in, "seq", split_axis=1, concat_axis=0, tiled=True)
    selector = (jnp.arange(count_mp) == place_mp).astype(jnp.float32)
    placed = grad_back.reshape(count_seq, 1, channels, rows_here) * selector[None, :, None, None]
    placed_rows = jnp.transpose(placed.reshape(model_width, rows_here))
    grad_normed = lax.psum(grad_normed_part + placed_rows, "mp")
    grad_tokens_norm, grad_gain1, grad_bias1 = norm1_pull(grad_normed)
    grad_tokens = grad_mixed + grad_tokens_norm
    feed_sums = sum_feed_grads(grad_up, grad_up_bias, grad_down, grad_down_bias)
    rest_sums = lax.psum(
        (grad_gain1, grad_bias1, grad_qkv, grad_out, grad_gain2, grad_bias2), "seq"
    )
    return (
        result,
        grad_tokens,
        rest_sums[0],
        rest_sums[1],
        grad_in_coef,
        grad_out_coef,
        grad_decay,
        grad_skip,
        rest_sums[2],
        rest_sums[3],
        rest_sums[4],
        rest_sums[5],
        feed_sums[0],
        feed_sums[1],
        feed_sums[2],
        feed_sums[3],
    )


def solution(mesh):
    placed = (
        P("seq", None),
        P(None, ("seq", "mp"), None),
        P(),
        P(),
        P(("seq", "mp"), None),
        P(("seq", "mp"), None),
        P(("seq", "mp"), None),
        P(("seq", "mp")),
        P(None, None, "mp"),
        P("mp", None),
        P(),
        P(),
        P(None, "mp"),
        P("mp"),
        P("mp", None),
        P(),
        P("seq", None),
    )
    return jax.shard_map(
        per_device,
        mesh=mesh,
        in_specs=placed,
        out_specs=(
            P("seq", None),
            P("seq", None),
            P(),
            P(),
            P(("seq", "mp"), None),
            P(("seq", "mp"), None),
            P(("seq", "mp"), None),
            P(("seq", "mp")),
            P(None, None, "mp"),
            P("mp", None),
            P(),
            P(),
            P(None, "mp"),
            P("mp"),
            P("mp", None),
            P(),
        ),
        check_vma=False,
    )
```

profile of v0, /device:TPU:0, one launch (start us, length us, event | category | flops | bytes accessed | tf_op | source)
XLA Modules:
  0.0 1192.9 jit_solution(4121227456708853096)
XLA Ops:
  15.8 7.4 all-to-all-start
  23.6 5.3 fusion.2
  39.0 7.2 all-to-all-done
  93.2 7.8 fusion.8
  105.9 31.6 %all_to_all.61 = f32[32,16,512]{2,0,1:T(8,128)} all-to-all(f32[32,16,512]{2,0,1:T(8,128)S(1)} %copy.94), channel_id=1, replica_groups=mesh['seq'=16,'mp'=2] {'seq'}, dimensions={1} | all-to-all | bytes 2097152 | tf_op jit(solution)/shard_map/all_to_all | solution.py:183
  155.1 16.1 %all-gather.3.cloned.1.call-done = f32[16,64,512]{2,1,0:T(8,128)} async-done(((f32[16,32,512]{2,1,0:T(8,128)}), f32[16,64,512]{2,1,0:T(8,128)}) %all-gather.3.cloned.1.call-update) | async-done | bytes 2097168 | tf_op jit(solution)/shard_map/all_gather | solution.py:185
  184.1 5.5 fusion.7
  192.0 6.4 fusion.28
  202.8 67.9 %all-reduce.21.cloned.1.call-done = f32[512,1024]{1,0:T(8,128)} async-done(((f32[512,1024]{1,0:T(8,128)}), f32[512,1024]{1,0:T(8,128)}) %all-reduce.21.cloned.1.call-update) | async-done | bytes 2097168 | tf_op jit(solution)/shard_map/psum | solution.py:199
  274.6 7.2 fusion.78
  281.9 19.5 %fusion.441 = (f32[2048]{0:T(1024)}, f32[512,2048]{1,0:T(8,128)S(1)}, f32[512,2048]{1,0:T(8,128)}) fusion(f32[512,2048]{1,0:T(8,128)S(1)} %fusion.78, f32[2048]{0:T(1024)S(1)} %copy-done.116, f32[512,1024]{1,0:T(8,128)S(1)} %copy-done.48, bf16[2048,1024]{1,0:T(8,128)(2,1)S(1)} %copy-done.125), kind=kOutput, calls=%fused_computation.500 | convolution fusion | flops 12961445888 | bytes 18890752 | tf_op jit(solution)/shard_map/transpose(jvp())/dot_general | solution.py:136
  303.4 8.0 fusion.450
  312.5 62.0 %all-reduce.23.cloned.1.call-done = f32[512,1024]{1,0:T(8,128)} async-done(((f32[512,1024]{1,0:T(8,128)}), f32[512,1024]{1,0:T(8,128)}) %all-reduce.23.cloned.1.call-update) | async-done | bytes 2097168 | tf_op jit(solution)/shard_map/psum | solution.py:206
  392.5 8.2 multiply_reduce_fusion.2
  416.8 68.0 %all-reduce.25.cloned.1.call-done = f32[16,2,32,512]{3,2,1,0:T(8,128)} async-done(((f32[16,2,32,512]{3,2,1,0:T(8,128)}), f32[16,2,32,512]{3,2,1,0:T(8,128)}) %all-reduce.25.cloned.1.call-update) | async-done | bytes 2097168
  486.8 30.3 %all_to_all.62 = f32[16,32,512]{2,1,0:T(8,128)S(1)} all-to-all(f32[16,32,512]{2,1,0:T(8,128)S(1)} %dynamic-slice_bitcast_fusion), channel_id=1, replica_groups=mesh['seq'=16,'mp'=2] {'seq'}, dimensions={0} | all-to-all | bytes 2097152 | tf_op jit(solution)/shard_map/all_to_all | solution.py:224
  536.6 5.0 multiply_reduce_fusion.4
  562.6 5.0 all-to-all-start.3
  567.8 12.2 %fusion.106 = f32[512,1024]{1,0:T(8,128)} fusion(bf16[2048,1024]{1,0:T(8,128)(2,1)} %param.31, f32[512,2048]{1,0:T(8,128)} %get-tuple-element.58, f32[512,2048]{1,0:T(8,128)} %copy-done.63, f32[2048]{0:T(1024)S(1)} %copy-done.117), kind=kOutput, calls=%fused_computation.157 | convolution fusion | flops 12888047616 | bytes 14688256 | tf_op jit(solution)/shard_map/dot_general | solution.py:136
  592.0 5.6 fusion.109
  602.3 8.1 bitcast_add_fusion
  612.0 17.8 %fusion.77 = f32[1024,2048]{1,0:T(8,128)} fusion(f32[512,2048]{1,0:T(8,128)} %copy-done.129, f32[512,1024]{1,0:T(8,128)S(1)} %copy-done.19, f32[1024]{0:T(1024)S(1)} %copy-done.127, f32[1024]{0:T(1024)S(1)} %copy-done.115, f32[512]{0:T(512)S(1)} %copy-done.99, f32[512]{0:T(512)S(1)} %copy-done.96), kind=kOutput, calls=%fused_computation.127 | convolution fusion | flops 12886999040 | bytes 14692352 | tf_op jit(solution)/shard_map/transpose(jvp())/dot_general | solution.py:135
  629.9 16.2 %fusion.105 = f32[2048,1024]{1,0:T(8,128)} fusion(f32[512,1024]{1,0:T(8,128)S(1)} %copy-done.50, f32[512,2048]{1,0:T(8,128)S(1)} %copy-done.65, f32[512,2048]{1,0:T(8,128)S(1)} %copy-done.64, f32[2048]{0:T(1024)S(1)} %copy-done.117), kind=kOutput, calls=%fused_computation.156 | convolution fusion | flops 12888047616 | bytes 18882560 | tf_op jit(solution)/shard_map/transpose(jvp())/dot_general | solution.py:136
  649.9 6.9 convolution_bitcast_fusion
  656.8 7.1 convolution_bitcast_fusion.1
  663.8 6.9 convolution_bitcast_fusion.2
  680.9 11.0 fusion.3
  700.9 11.1 fusion
  712.1 10.6 multiply_reduce_fusion.1
  728.6 65.8 %all-reduce.12 = (f32[1024]{0:T(1024)}, f32[1024]{0:T(1024)}, f32[1024]{0:T(1024)}, f32[1024]{0:T(1024)}, f32[2048]{0:T(1024)}, /*index=5*/f32[1024]{0:T(1024)}) all-reduce(f32[1024]{0:T(1024)S(1)} %get-tuple-element.36, f32[1024]{0:T(1024)S(1)} %get-tuple-element.43, ...), channel_id=1, replica_groups=mesh['seq'=16,'mp'=2] {'seq'}, use_global_device_ids=true, to_apply=%region_17.18 | all-reduce | flops 7168 | bytes 57344 | tf_op jit(solution)/shard_map/psum | solution.py:240
  801.7 366.3 %all-reduce.27.cloned.1.call-done = (f32[3,1024,512]{2,1,0:T(8,128)}, f32[512,1024]{1,0:T(8,128)}, f32[1024,2048]{1,0:T(8,128)}, f32[2048,1024]{1,0:T(8,128)}) async-done(((f32[3,1024,512]{2,1,0:T(8,128)}, f32[512,1024]{1,0:T(8,128)}, f32[1024,2048]{1,0:T(8,128)}, f32[2048,1024]{1,0:T(8,128)}), (f32[3,1024,512]{2,1,0:T(8,128)}, f32[512,1024]{1,0:T(8,128)}, f32[1024,2048]{1,0:T(8,128)}, ...) | async-done | bytes 25165840 | tf_op jit(solution)/shard_map/psum | solution.py:240
  1168.0 6.9 copy.162
  (441 shorter events, 255.5 us)
Async XLA Ops:
  7.2 192.2 %copy-start = (bf16[512,1024]{1,0:T(8,128)(2,1)S(1)}, bf16[512,1024]{1,0:T(8,128)(2,1)}, u32[]{:S(2)}) copy-start(bf16[512,1024]{1,0:T(8,128)(2,1)} %param.26) | copy-start | bytes 3145732
  11.4 166.0 %copy-start.2 = (f32[512,1024]{1,0:T(8,128)}, f32[512,1024]{1,0:T(8,128)S(1)}, u32[]{:S(2)}) copy-start(f32[512,1024]{1,0:T(8,128)S(1)} %multiply_add_fusion.6) | copy-start | bytes 6291460
  15.8 30.4 %all-to-all-start = ((f32[16,32,512]{2,1,0:T(8,128)}), f32[16,32,512]{2,1,0:T(8,128)}, u32[]{:S(2)}, u32[]{:S(2)}) async-start(f32[16,32,512]{2,1,0:T(8,128)} %dynamic-slice_bitcast_fusion.1), calls=%async_computation | async-start | bytes 2097152 | tf_op jit(solution)/shard_map/all_to_all | solution.py:177
  23.2 147.9 %all-gather.3.cloned.1.call-start = ((), (), s32[]{:S(2)}) async-start(), calls=%async_computation.6 | async-start | bytes 3145728 | tf_op jit(solution)/shard_map/all_gather | solution.py:185
  23.3 69.9 %copy-start.109 = (f32[4096]{0:T(1024)}, f32[4096]{0:T(1024)S(1)}, u32[]{:S(2)}) copy-start(f32[4096]{0:T(1024)S(1)} %iota_convert_fusion) | copy-start | bytes 49156
  23.4 69.8 %copy-start.90 = (f32[2,32,16]{2,0,1:T(2,128)}, f32[2,32,16]{2,0,1:T(2,128)S(1)}, u32[]{:S(2)}) copy-start(f32[2,32,16]{2,0,1:T(2,128)S(1)} %copy.93) | copy-start | bytes 12292
  23.5 69.7 %copy-start.105 = (f32[32,16]{1,0:T(8,128)}, f32[32,16]{1,0:T(8,128)S(1)}, u32[]{:S(2)}) copy-start(f32[32,16]{1,0:T(8,128)S(1)} %get-tuple-element.72) | copy-start | bytes 6148
  23.5 69.7 %copy-start.107 = (f32[32,16]{1,0:T(8,128)}, f32[32,16]{1,0:T(8,128)S(1)}, u32[]{:S(2)}) copy-start(f32[32,16]{1,0:T(8,128)S(1)} %get-tuple-element.73) | copy-start | bytes 6148
  137.6 133.1 %all-reduce.21.cloned.1.call-start = ((), (), s32[]{:S(2)}) async-start(), calls=%async_computation.4 | async-start | bytes 4194304 | tf_op jit(solution)/shard_map/psum | solution.py:199
  175.2 4.1 collective-permute-start
  202.5 68.1 %copy-start.11 = (f32[512,1024]{1,0:T(8,128)S(1)}, f32[512,1024]{1,0:T(8,128)}, u32[]{:S(2)}) copy-start(f32[512,1024]{1,0:T(8,128)} %param.17) | copy-start | bytes 6291460
  202.6 172.0 %all-reduce.23.cloned.1.call-start = ((), (), s32[]{:S(2)}) async-start(), calls=%async_computation.5 | async-start | bytes 4194304 | tf_op jit(solution)/shard_map/psum | solution.py:206
  281.9 19.5 %copy-start.63 = (f32[512,2048]{1,0:T(8,128)}, f32[512,2048]{1,0:T(8,128)S(1)}, u32[]{:S(2)}) copy-start(f32[512,2048]{1,0:T(8,128)S(1)} %fusion.78) | copy-start | bytes 12582916
  311.4 63.1 %copy-start.18 = (f32[512,1024]{1,0:T(8,128)S(1)}, f32[512,1024]{1,0:T(8,128)}, u32[]{:S(2)}) copy-start(f32[512,1024]{1,0:T(8,128)} %copy-done.17) | copy-start | bytes 6291460
  311.5 173.4 %all-reduce.25.cloned.1.call-start = ((), (), s32[]{:S(2)}) async-start(), calls=%async_computation.7 | async-start | bytes 4194304
  409.8 3.8 collective-permute-start.1
  562.6 35.0 %all-to-all-start.3 = ((f32[32,16,512]{2,0,1:T(8,128)}), f32[32,16,512]{2,0,1:T(8,128)S(1)}, u32[]{:S(2)}, u32[]{:S(2)}) async-start(f32[32,16,512]{2,0,1:T(8,128)} %copy.107), calls=%async_computation.3 | async-start | bytes 2097152 | tf_op jit(solution)/shard_map/all_to_all | solution.py:232
  567.6 158.5 %all-reduce.29.cloned.1.call-start = ((), (), s32[]{:S(2)}) async-start(), calls=%async_computation.9 | async-start | bytes 8388608 | tf_op jit(solution)/shard_map/psum | solution.py:202
  567.8 12.2 %copy-start.74 = (f32[1,640,4,128]{1,3,2,0:T(8,128)S(1)}, f32[1,640,4,128]{1,3,2,0:T(8,128)}, u32[]{:S(2)}) copy-start(f32[1,640,4,128]{1,3,2,0:T(8,128)} %copy-done.73) | copy-start | bytes 3932164
  567.8 12.3 %copy-start.56 = (f32[1,640,4,128]{1,3,2,0:T(8,128)S(1)}, f32[1,640,4,128]{1,3,2,0:T(8,128)}, u32[]{:S(2)}) copy-start(f32[1,640,4,128]{1,3,2,0:T(8,128)} %copy-done.55) | copy-start | bytes 3932164
  580.1 11.8 slice-start.4
  610.5 557.5 %all-reduce.27.cloned.1.call-start = ((), (), s32[]{:S(2)}) async-start(), calls=%async_computation.8 | async-start | bytes 50331648 | tf_op jit(solution)/shard_map/psum | solution.py:240
  612.0 17.8 %copy-start.50 = (f32[512,1024]{1,0:T(8,128)S(1)}, f32[512,1024]{1,0:T(8,128)}, u32[]{:S(2)}) copy-start(f32[512,1024]{1,0:T(8,128)} %param.33) | copy-start | bytes 6291460
  612.0 17.8 %copy-start.64 = (f32[512,2048]{1,0:T(8,128)S(1)}, f32[512,2048]{1,0:T(8,128)}, u32[]{:S(2)}) copy-start(f32[512,2048]{1,0:T(8,128)} %copy-done.63) | copy-start | bytes 12582916
  612.0 17.8 %copy-start.65 = (f32[512,2048]{1,0:T(8,128)S(1)}, f32[512,2048]{1,0:T(8,128)}, u32[]{:S(2)}) copy-start(f32[512,2048]{1,0:T(8,128)} %get-tuple-element.58) | copy-start | bytes 12582916
  629.9 16.2 %copy-start.53 = (f32[1024,1,512]{0,2,1:T(8,128)S(1)}, f32[1024,1,512]{0,2,1:T(8,128)}, u32[]{:S(2)}) copy-start(f32[1024,1,512]{0,2,1:T(8,128)} %copy-done.52) | copy-start | bytes 6291460
  680.9 11.1 copy-start.28
  680.9 11.1 copy-start.29
  700.9 11.2 copy-start.91
  712.1 11.4 copy-start.83
  712.1 11.4 copy-start.31
  726.2 68.2 %copy-start.101 = (f32[512]{0:T(512)S(1)}, f32[512]{0:T(512)}, u32[]{:S(2)}) copy-start(f32[512]{0:T(512)} %copy-done.100) | copy-start | bytes 6148
  (116 other events, 427.6 us)
Sparse Core Ops, SparseCore 0:
  137.7 33.4 all-gather.2
  202.7 67.9 all-reduce.20
  311.6 62.9 all-reduce.22
  415.7 69.0 all-reduce.24
  610.6 108.5 all-reduce.28
  724.5 443.4 all-reduce.26
where the time goes:
time: 1200 us; the launch traced here: 1190 us
  waiting for transfers between devices  590 us (49%)
  matrix products  308 us (26%)
  blocking collectives  128 us (11%)
  local copies, waits for them, and re-layouts  99.9 us (8%)
  other arithmetic  34.4 us (3%)
  starting transfers between devices  16.5 us (1%)
  between operations  16.5 us (1%)
    psum x1, waiting for transfers between devices, per_device(): lax.psum((grad_gain1, grad_bias1, grad_qkv, grad_out, grad_gain2, grad_bi...  366 us
    dot_general x50, matrix products, product(): return jnp.einsum(form, left, right, precision=lax.Precision.HIGHEST)  140 us
    unnamed x7, waiting for transfers between devices  68.1 us
    psum x1, waiting for transfers between devices, per_device(): mixed = tokens + lax.psum(attn_part, 'mp')  67.9 us
    psum x1, blocking collectives, per_device(): lax.psum((grad_gain1, grad_bias1, grad_qkv, grad_out, grad_gain2, grad_bi...  65.8 us
    psum x1, waiting for transfers between devices, per_device(): grad_normed2 = lax.psum(grad_normed2_part, 'mp')  62 us
    dot_general x3, matrix products, feed_local(): return jnp.dot(hidden, down_w, precision=highest)  47.9 us
    unnamed x287, local copies, waits for them, and re-layouts  37.9 us
  transfers between devices with their start and end apart: 10, of which 7 were waited for; matrix products, arithmetic and copies ran while one was open for 15% of the time, Pallas kernels for 0%

commit v1 on v0

--- a/solution.py
+++ b/solution.py
@@ -9,6 +9,30 @@
 CTX = 128
 LEN = 4096
 epsilon = 1e-05
+
+
+def split_up(x, dim, devices):
+    shape = x.shape
+    pieces = x.reshape(*shape[:dim], devices, shape[dim] // devices, *shape[dim + 1 :])
+    return jnp.moveaxis(pieces, dim, 0)
+
+
+def joined_along(pieces, dim):
+    shape = list(pieces.shape[1:])
+    shape[dim] *= pieces.shape[0]
+    return jnp.moveaxis(pieces, 0, dim).reshape(shape)
+
+
+def sent_to_each(x, axis, split_dim, concat_dim):
+    size, index = (lax.axis_size(axis), lax.axis_index(axis))
+    tiles = split_up(x, split_dim, size)
+    out = tiles
+    for turn in range(1, size):
+        target, source = ((index + turn) % size, (index - turn) % size)
+        sent = lax.dynamic_index_in_dim(tiles, target, 0)
+        other = lax.ppermute(sent, axis, [(i, (i + turn) % size) for i in range(size)])
+        out = lax.dynamic_update_slice_in_dim(out, other, source, axis=0)
+    return joined_along(out, concat_dim)
 
 
 def from_behind(block, axis, distance):
@@ -180,7 +204,7 @@
         return ssm_local(time_rows, coef_in, coef_out, rates, skips, window_state)
 
     time_out, ssm_pull = jax.vjp(ssm_piece, time_in, in_coef, out_coef, decay_rate, skip_gain)
-    returned = lax.all_to_all(time_out, "seq", split_axis=1, concat_axis=0, tiled=True)
+    returned = sent_to_each(time_out, "seq", 1, 0)
     width_back = returned.shape[1]
     halves = lax.all_gather(
         returned.reshape(count_seq, 1, channels, width_back), "mp", axis=1, tiled=True

time: 1200 us -> 1220 us (1.017)
  blocking collectives: 128 us -> 95.9 us
  starting transfers between devices: 16.5 us -> 41.7 us
  local copies, waits for them, and re-layouts: 99.9 us -> 125 us
    all_to_all x1 -> x0, blocking collectives: 31.6 us -> none  [per_device(): lax.all_to_all(time_out, 'seq', split_axis=1, concat_axis=0, tiled=True)]
    ppermute x0 -> x15, starting transfers between devices: none -> 25.3 us  [sent_to_each(): lax.ppermute(sent, axis, [(i, (i + turn) % size) for i in range(size)])]
    unnamed x287 -> x322, local copies, waits for them, and re-layouts: 37.9 us -> 40.9 us
  transfers between devices with their start and end apart: 10 -> 25, of which waited for: 7 -> 7; matrix products, arithmetic and copies ran while one was open for 15% -> 16% of each run, Pallas kernels for 0% -> 0%
where the time goes in v1:
time: 1220 us; the launch traced here: 1210 us
  waiting for transfers between devices  588 us (48%)
  matrix products  308 us (25%)
  local copies, waits for them, and re-layouts  125 us (10%)
  blocking collectives  95.9 us (8%)
  starting transfers between devices  41.7 us (3%)
  other arithmetic  38.1 us (3%)
  between operations  16.7 us (1%)
    psum x1, waiting for transfers between devices, per_device(): lax.psum((grad_gain1, grad_bias1, grad_qkv, grad_out, grad_gain2, grad_bi...  367 us
    dot_general x50, matrix products, product(): return jnp.einsum(form, left, right, precision=lax.Precision.HIGHEST)  141 us
    unnamed x7, waiting for transfers between devices  68.1 us
    psum x1, waiting for transfers between devices, per_device(): mixed = tokens + lax.psum(attn_part, 'mp')  67.9 us
    psum x1, blocking collectives, per_device(): lax.psum((grad_gain1, grad_bias1, grad_qkv, grad_out, grad_gain2, grad_bi...  65.6 us
    psum x1, waiting for transfers between devices, per_device(): grad_normed2 = lax.psum(grad_normed2_part, 'mp')  62.2 us
    dot_general x3, matrix products, feed_local(): return jnp.dot(hidden, down_w, precision=highest)  47.2 us
    unnamed x322, local copies, waits for them, and re-layouts  40.9 us
  transfers between devices with their start and end apart: 25, of which 7 were waited for; matrix products, arithmetic and copies ran while one was open for 16% of the time, Pallas kernels for 0%

profile of v1, /device:TPU:0, one launch (start us, length us, event | category | flops | bytes accessed | tf_op | source)
XLA Modules:
  0.0 1213.3 jit_solution(5934348725218581919)
XLA Ops:
  15.8 7.4 all-to-all-start
  23.8 5.4 fusion.2
  93.5 7.8 fusion.8
  104.4 5.6 constant_dynamic-slice_fusion
  167.1 15.6 %all-gather.2.cloned.1.call-done = f32[16,2,32,512]{3,2,1,0:T(8,128)} async-done(((f32[16,1,32,512]{3,2,1,0:T(8,128)}), f32[16,2,32,512]{3,2,1,0:T(8,128)}) %all-gather.2.cloned.1.call-update) | async-done | bytes 2097168 | tf_op jit(solution)/shard_map/all_gather | solution.py:209
  195.5 5.5 fusion.7
  203.3 6.3 fusion.28
  214.2 67.9 %all-reduce.21.cloned.1.call-done = f32[512,1024]{1,0:T(8,128)} async-done(((f32[512,1024]{1,0:T(8,128)}), f32[512,1024]{1,0:T(8,128)}) %all-reduce.21.cloned.1.call-update) | async-done | bytes 2097168 | tf_op jit(solution)/shard_map/psum | solution.py:223
  286.0 7.2 fusion.78
  293.3 19.4 %fusion.441 = (f32[2048]{0:T(1024)}, f32[512,2048]{1,0:T(8,128)S(1)}, f32[512,2048]{1,0:T(8,128)}) fusion(f32[512,2048]{1,0:T(8,128)S(1)} %fusion.78, f32[2048]{0:T(1024)S(1)} %copy-done.128, f32[512,1024]{1,0:T(8,128)S(1)} %copy-done.52, bf16[2048,1024]{1,0:T(8,128)(2,1)S(1)} %copy-done.137), kind=kOutput, calls=%fused_computation.546 | convolution fusion | flops 12961445888 | bytes 18890752 | tf_op jit(solution)/shard_map/transpose(jvp())/dot_general | solution.py:160
  314.7 8.0 fusion.450
  323.6 62.2 %all-reduce.23.cloned.1.call-done = f32[512,1024]{1,0:T(8,128)} async-done(((f32[512,1024]{1,0:T(8,128)}), f32[512,1024]{1,0:T(8,128)}) %all-reduce.23.cloned.1.call-update) | async-done | bytes 2097168 | tf_op jit(solution)/shard_map/psum | solution.py:230
  403.6 8.8 multiply_reduce_fusion.2
  431.7 68.0 %all-reduce.25.cloned.1.call-done = f32[16,2,32,512]{3,2,1,0:T(8,128)} async-done(((f32[16,2,32,512]{3,2,1,0:T(8,128)}), f32[16,2,32,512]{3,2,1,0:T(8,128)}) %all-reduce.25.cloned.1.call-update) | async-done | bytes 2097168
  501.7 30.3 %all_to_all.45 = f32[16,32,512]{2,1,0:T(8,128)S(1)} all-to-all(f32[16,32,512]{2,1,0:T(8,128)S(1)} %dynamic-slice_bitcast_fusion), channel_id=1, replica_groups=mesh['seq'=16,'mp'=2] {'seq'}, dimensions={0} | all-to-all | bytes 2097152 | tf_op jit(solution)/shard_map/all_to_all | solution.py:248
  551.4 5.0 multiply_reduce_fusion.4
  580.5 5.0 all-to-all-start.2
  585.8 11.9 fusion.106
  605.2 4.9 fusion.116
  610.2 6.6 fusion.109
  622.8 8.1 bitcast_add_fusion
  632.6 17.8 %fusion.77 = f32[1024,2048]{1,0:T(8,128)} fusion(f32[512,2048]{1,0:T(8,128)} %copy-done.141, f32[512,1024]{1,0:T(8,128)S(1)} %copy-done.19, f32[1024]{0:T(1024)S(1)} %copy-done.139, f32[1024]{0:T(1024)S(1)} %copy-done.127, f32[512]{0:T(512)S(1)} %copy-done.111, f32[512]{0:T(512)S(1)} %copy-done.108), kind=kOutput, calls=%fused_computation.127 | convolution fusion | flops 12886999040 | bytes 14692352 | tf_op jit(solution)/shard_map/transpose(jvp())/dot_general | solution.py:159
  650.4 16.0 %fusion.105 = f32[2048,1024]{1,0:T(8,128)} fusion(f32[512,1024]{1,0:T(8,128)S(1)} %copy-done.54, f32[512,2048]{1,0:T(8,128)S(1)} %copy-done.68, f32[512,2048]{1,0:T(8,128)S(1)} %copy-done.67, f32[2048]{0:T(1024)S(1)} %copy-done.129), kind=kOutput, calls=%fused_computation.156 | convolution fusion | flops 12888047616 | bytes 18882560 | tf_op jit(solution)/shard_map/transpose(jvp())/dot_general | solution.py:160
  670.1 6.7 convolution_bitcast_fusion
  676.8 7.1 convolution_bitcast_fusion.1
  683.9 6.7 convolution_bitcast_fusion.2
  700.6 11.0 fusion.3
  720.7 11.3 fusion
  732.1 10.6 multiply_reduce_fusion.1
  748.6 65.6 %all-reduce.12 = (f32[1024]{0:T(1024)}, f32[1024]{0:T(1024)}, f32[1024]{0:T(1024)}, f32[1024]{0:T(1024)}, f32[2048]{0:T(1024)}, /*index=5*/f32[1024]{0:T(1024)}) all-reduce(f32[1024]{0:T(1024)S(1)} %get-tuple-element.36, f32[1024]{0:T(1024)S(1)} %get-tuple-element.43, ...), channel_id=1, replica_groups=mesh['seq'=16,'mp'=2] {'seq'}, use_global_device_ids=true, to_apply=%region_17.18 | all-reduce | flops 7168 | bytes 57344 | tf_op jit(solution)/shard_map/psum | solution.py:264
  821.5 366.9 %all-reduce.27.cloned.1.call-done = (f32[3,1024,512]{2,1,0:T(8,128)}, f32[512,1024]{1,0:T(8,128)}, f32[1024,2048]{1,0:T(8,128)}, f32[2048,1024]{1,0:T(8,128)}) async-done(((f32[3,1024,512]{2,1,0:T(8,128)}, f32[512,1024]{1,0:T(8,128)}, f32[1024,2048]{1,0:T(8,128)}, f32[2048,1024]{1,0:T(8,128)}), (f32[3,1024,512]{2,1,0:T(8,128)}, f32[512,1024]{1,0:T(8,128)}, f32[1024,2048]{1,0:T(8,128)}, ...) | async-done | bytes 25165840 | tf_op jit(solution)/shard_map/psum | solution.py:264
  1188.5 6.9 copy.224
  (520 shorter events, 303.1 us)
Async XLA Ops:
  7.2 203.4 %copy-start = (bf16[512,1024]{1,0:T(8,128)(2,1)S(1)}, bf16[512,1024]{1,0:T(8,128)(2,1)}, u32[]{:S(2)}) copy-start(bf16[512,1024]{1,0:T(8,128)(2,1)} %param.26) | copy-start | bytes 3145732
  11.4 177.4 %copy-start.2 = (f32[512,1024]{1,0:T(8,128)}, f32[512,1024]{1,0:T(8,128)S(1)}, u32[]{:S(2)}) copy-start(f32[512,1024]{1,0:T(8,128)S(1)} %multiply_add_fusion.6) | copy-start | bytes 6291460
  15.8 30.4 %all-to-all-start = ((f32[16,32,512]{2,1,0:T(8,128)}), f32[16,32,512]{2,1,0:T(8,128)}, u32[]{:S(2)}, u32[]{:S(2)}) async-start(f32[16,32,512]{2,1,0:T(8,128)} %dynamic-slice_bitcast_fusion.1), calls=%async_computation | async-start | bytes 2097152 | tf_op jit(solution)/shard_map/all_to_all | solution.py:201
  23.2 159.5 %all-gather.2.cloned.1.call-start = ((), (), s32[]{:S(2)}) async-start(), calls=%async_computation.3 | async-start | bytes 3145728 | tf_op jit(solution)/shard_map/all_gather | solution.py:209
  23.3 70.1 %copy-start.121 = (f32[4096]{0:T(1024)}, f32[4096]{0:T(1024)S(1)}, u32[]{:S(2)}) copy-start(f32[4096]{0:T(1024)S(1)} %iota_convert_fusion) | copy-start | bytes 49156
  23.6 69.8 %copy-start.102 = (f32[2,32,16]{2,0,1:T(2,128)}, f32[2,32,16]{2,0,1:T(2,128)S(1)}, u32[]{:S(2)}) copy-start(f32[2,32,16]{2,0,1:T(2,128)S(1)} %copy.93) | copy-start | bytes 12292
  23.7 69.7 %copy-start.117 = (f32[32,16]{1,0:T(8,128)}, f32[32,16]{1,0:T(8,128)S(1)}, u32[]{:S(2)}) copy-start(f32[32,16]{1,0:T(8,128)S(1)} %get-tuple-element.87) | copy-start | bytes 6148
  23.7 69.7 %copy-start.119 = (f32[32,16]{1,0:T(8,128)}, f32[32,16]{1,0:T(8,128)S(1)}, u32[]{:S(2)}) copy-start(f32[32,16]{1,0:T(8,128)S(1)} %get-tuple-element.88) | copy-start | bytes 6148
  110.6 10.3 collective-permute-start
  114.2 10.6 collective-permute-start.1
  116.2 12.1 %collective-permute-start.2 = (f32[1,32,512]{2,1,0:T(8,128)S(1)}, f32[1,32,512]{2,1,0:T(8,128)S(1)}, u32[]{:S(2)}, u32[]{:S(2)}) collective-permute-start(f32[1,32,512]{2,1,0:T(8,128)S(1)} %bitcast.537), channel_id=1, source_target_pairs={{0,6},{2,8},{4,10},{6,12},{8,14},{10,16},{12,18},{14,20},{16,22},{... | collective-permute-start | bytes 196616 | tf_op jit(solution)/shard_map/ppermute | solution.py:33
  119.8 10.2 collective-permute-start.3
  120.6 11.0 collective-permute-start.4
  120.9 12.6 %collective-permute-start.5 = (f32[1,32,512]{2,1,0:T(8,128)S(1)}, f32[1,32,512]{2,1,0:T(8,128)S(1)}, u32[]{:S(2)}, u32[]{:S(2)}) collective-permute-start(f32[1,32,512]{2,1,0:T(8,128)S(1)} %bitcast.534), channel_id=1, source_target_pairs={{0,12},{2,14},{4,16},{6,18},{8,20},{10,22},{12,24},{14,26},{16,28}... | collective-permute-start | bytes 196616 | tf_op jit(solution)/shard_map/ppermute | solution.py:33
  124.8 12.5 %collective-permute-start.6 = (f32[1,32,512]{2,1,0:T(8,128)S(1)}, f32[1,32,512]{2,1,0:T(8,128)S(1)}, u32[]{:S(2)}, u32[]{:S(2)}) collective-permute-start(f32[1,32,512]{2,1,0:T(8,128)S(1)} %bitcast.533), channel_id=1, source_target_pairs={{0,14},{2,16},{4,18},{6,20},{8,22},{10,24},{12,26},{14,28},{16,30}... | collective-permute-start | bytes 196616 | tf_op jit(solution)/shard_map/ppermute | solution.py:33
  128.3 11.1 collective-permute-start.7
  130.0 10.4 collective-permute-start.8
  131.6 10.6 collective-permute-start.9
  133.5 12.7 %collective-permute-start.10 = (f32[1,32,512]{2,1,0:T(8,128)S(1)}, f32[1,32,512]{2,1,0:T(8,128)S(1)}, u32[]{:S(2)}, u32[]{:S(2)}) collective-permute-start(f32[1,32,512]{2,1,0:T(8,128)S(1)} %bitcast.529), channel_id=1, source_target_pairs={{0,22},{2,24},{4,26},{6,28},{8,30},{10,0},{12,2},{14,4},{16,6},{18... | collective-permute-start | bytes 196616 | tf_op jit(solution)/shard_map/ppermute | solution.py:33
  137.3 9.6 collective-permute-start.11
  139.5 8.1 collective-permute-start.12
  140.4 7.8 collective-permute-start.13
  142.2 6.6 collective-permute-start.14
  149.5 132.6 %all-reduce.21.cloned.1.call-start = ((), (), s32[]{:S(2)}) async-start(), calls=%async_computation.4 | async-start | bytes 4194304 | tf_op jit(solution)/shard_map/psum | solution.py:223
  186.8 3.9 collective-permute-start.15
  213.7 68.4 %copy-start.11 = (f32[512,1024]{1,0:T(8,128)S(1)}, f32[512,1024]{1,0:T(8,128)}, u32[]{:S(2)}) copy-start(f32[512,1024]{1,0:T(8,128)} %param.17) | copy-start | bytes 6291460
  213.7 172.1 %all-reduce.23.cloned.1.call-start = ((), (), s32[]{:S(2)}) async-start(), calls=%async_computation.5 | async-start | bytes 4194304 | tf_op jit(solution)/shard_map/psum | solution.py:230
  322.7 177.0 %all-reduce.25.cloned.1.call-start = ((), (), s32[]{:S(2)}) async-start(), calls=%async_computation.6 | async-start | bytes 4194304
  422.2 3.8 collective-permute-start.16
  580.5 36.2 %all-to-all-start.2 = ((f32[32,16,512]{2,0,1:T(8,128)}), f32[32,16,512]{2,0,1:T(8,128)}, u32[]{:S(2)}, u32[]{:S(2)}) async-start(f32[32,16,512]{2,0,1:T(8,128)} %copy.107), calls=%async_computation.2 | async-start | bytes 2097152 | tf_op jit(solution)/shard_map/all_to_all | solution.py:256
  585.5 160.6 %all-reduce.29.cloned.1.call-start = ((), (), s32[]{:S(2)}) async-start(), calls=%async_computation.8 | async-start | bytes 8388608 | tf_op jit(solution)/shard_map/psum | solution.py:226
  631.0 557.5 %all-reduce.27.cloned.1.call-start = ((), (), s32[]{:S(2)}) async-start(), calls=%async_computation.7 | async-start | bytes 50331648 | tf_op jit(solution)/shard_map/psum | solution.py:264
  (141 other events, 810.6 us)
Sparse Core Ops, SparseCore 0:
  149.6 33.0 all-gather.1
  213.9 68.1 all-reduce.20
  322.8 62.9 all-reduce.22
  430.6 69.0 all-reduce.24
  631.1 108.5 all-reduce.28
  745.0 443.4 all-reduce.26
